TPU v7x, 128 devices: a whole 4x4x4 slice. The times are simulated.
128 devices in a mesh: gx: 8 (over y, core), gy: 4 (over z), gz: 4 (over x).
Axes of the slice: x: 4, y: 4, z: 4, core: 2. Of those that a mesh axis runs over, the one named last changes fastest.
Arguments:
- right_side: float32 [128, 64, 1024], P('gx', 'gy', 'gz'), may hold values from -8 to 8
- conductance: float32 [3, 128, 64, 1024], P(None, 'gx', 'gy', 'gz'), may hold values from 0.2 to 5
- storage: float32 [128, 64, 1024], P('gx', 'gy', 'gz'), may hold values from 0.05 to 0.8
- dirichlet: int32 [128, 64, 1024], P('gx', 'gy', 'gz'), may hold values 0 or 1
- basis: float32 [16, 128, 64, 1024], P(None, 'gx', 'gy', 'gz'), may hold values from -2 to 2
- coarse_inverse: float32 [2048, 2048], P(('gx', 'gy', 'gz')), may hold values from 0 to 2, as said below
Outputs:
- solution_field: float32 [128, 64, 1024], P('gx', 'gy', 'gz')
- residual: float32 [128, 64, 1024], P('gx', 'gy', 'gz')
Inputs may be any that keep to these rules, and one draw needn't show every extreme that they name: `coarse_inverse`: symmetric positive definite.
All inputs are finite; a program needn't handle non-finite values. No bound on the sum of `dirichlet` on one device may be relied on, other than what follows from the above.
Results may differ from a plain program's by a relative error of at most 0.0003.
Values sent between devices are 32-bit elements; how exact they have to be, the bound alone decides.
A program may use at most 128 MiB of HBM per device.

v0:
```python
import jax
import jax.numpy as jnp
from jax import lax
from jax.sharding import PartitionSpec as P

SWEEPS = 4
ITERS = 2


RELAX = 2.0 / 3.0


def padded(value, sides, width):
    for axis, dim in sides:
        count, length = (lax.axis_size(axis), value.shape[dim])
        up = [(i, (i + 1) % count) for i in range(count - 1)]
        down = [(j, i) for i, j in up]
        last = lax.slice_in_dim(value, length - width, length, axis=dim)
        leading = lax.slice_in_dim(value, 0, width, axis=dim)
        before = lax.ppermute(last, axis, up)
        after = lax.ppermute(leading, axis, down)
        value = jnp.concatenate([before, value, after], axis=dim)
    return value


def pad_cond(cond):
    return jnp.pad(cond, ((0, 0), (1, 1), (1, 1), (1, 1)))


def stencil(padded_free, padded_cond, field, storage, free):
    middle = padded_free[1:-1, 1:-1, 1:-1]
    total = storage * middle
    total = (
        total
        + padded_cond[0, 1:-1, 1:-1, 1:-1] * (middle - padded_free[2:, 1:-1, 1:-1])
        + padded_cond[0, :-2, 1:-1, 1:-1] * (middle - padded_free[:-2, 1:-1, 1:-1])
    )
    total = (
        total
        + padded_cond[1, 1:-1, 1:-1, 1:-1] * (middle - padded_free[1:-1, 2:, 1:-1])
        + padded_cond[1, 1:-1, :-2, 1:-1] * (middle - padded_free[1:-1, :-2, 1:-1])
    )
    total = (
        total
        + padded_cond[2, 1:-1, 1:-1, 1:-1] * (middle - padded_free[1:-1, 1:-1, 2:])
        + padded_cond[2, 1:-1, 1:-1, :-2] * (middle - padded_free[1:-1, 1:-1, :-2])
    )
    return free * total + (1.0 - free) * field


def diagonal_of(padded_cond, storage, free):
    total = storage + padded_cond[0, 1:-1, 1:-1, 1:-1] + padded_cond[0, :-2, 1:-1, 1:-1]
    total = total + padded_cond[1, 1:-1, 1:-1, 1:-1] + padded_cond[1, 1:-1, :-2, 1:-1]
    total = total + padded_cond[2, 1:-1, 1:-1, 1:-1] + padded_cond[2, 1:-1, 1:-1, :-2]
    return free * total + (1.0 - free)


def jacobi(rhs_box, padded_cond, diagonal, storage_box, free_box):
    guess = jnp.zeros_like(rhs_box)
    for sweep in range(SWEEPS):
        image = stencil(jnp.pad(free_box * guess, 1), padded_cond, guess, storage_box, free_box)
        guess = guess + RELAX * (rhs_box - image) / diagonal
    return guess


def project(basis, field):
    return jnp.dot(
        basis.reshape(basis.shape[0], -1), field.reshape(-1), precision=lax.Precision.HIGHEST
    )


def expand(basis, weights, field):
    return jnp.dot(
        weights, basis.reshape(basis.shape[0], -1), precision=lax.Precision.HIGHEST
    ).reshape(field.shape)


def gather_coarse(values):
    return lax.all_gather(values, ("gx", "gy", "gz"), axis=0, tiled=True)


def residual_rim(field):
    return padded(field, (("gx", 0), ("gy", 1), ("gz", 2)), 2)


def norm_sum(value):
    return lax.psum(value, ("gx", "gy", "gz"))


def shards(right_side, conductance, storage, dirichlet, basis, coarse_inverse):
    free = 1.0 - dirichlet.astype(jnp.float32)
    stacked = jnp.concatenate([conductance, storage[None], free[None]], axis=0)
    wide = padded(stacked, (("gx", 1), ("gy", 2), ("gz", 3)), 3)
    cond_face = wide[:3, 2:-2, 2:-2, 2:-2]
    free_face = wide[4, 2:-2, 2:-2, 2:-2]
    cond_box = wide[:3, 1:-1, 1:-1, 1:-1]
    storage_box = wide[3, 1:-1, 1:-1, 1:-1]
    free_box = wide[4, 1:-1, 1:-1, 1:-1]
    box_cond = pad_cond(cond_box)
    box_diag = diagonal_of(box_cond, storage_box, free_box)

    def schwarz(rhs_box):
        return jacobi(rhs_box, box_cond, box_diag, storage_box, free_box)[2:-2, 2:-2, 2:-2]

    solution = jnp.zeros_like(right_side)
    residual = right_side
    rhs_box = residual_rim(residual)
    coarse_now = project(basis, residual)
    weights = jnp.dot(coarse_inverse, gather_coarse(coarse_now), precision=lax.Precision.HIGHEST)
    precond = schwarz(rhs_box) + expand(basis, weights, residual)
    norm_now = norm_sum(jnp.sum(residual * precond))
    direction = precond
    for step in range(ITERS):
        near_dir = padded(direction, (("gx", 0), ("gy", 1), ("gz", 2)), 1)
        image = stencil(free_face * near_dir, cond_face, direction, storage, free)
        local_curve = jnp.sum(direction * image)
        curvature = lax.psum(local_curve, ("gx", "gy", "gz"))
        alpha = norm_now / curvature
        solution = solution + alpha * direction
        residual = residual - alpha * image
        if step + 1 < ITERS:
            rhs_box = residual_rim(residual)
            coarse_now = project(basis, residual)
            gathered = gather_coarse(coarse_now)
            weights = jnp.dot(coarse_inverse, gathered, precision=lax.Precision.HIGHEST)
            precond = schwarz(rhs_box) + expand(basis, weights, residual)
            norm_next = norm_sum(jnp.sum(residual * precond))
            direction = precond + norm_next / norm_now * direction
            norm_now = norm_next
    return (solution, residual)


def solution(mesh):
    placed = (
        P("gx", "gy", "gz"),
        P(None, "gx", "gy", "gz"),
        P("gx", "gy", "gz"),
        P("gx", "gy", "gz"),
        P(None, "gx", "gy", "gz"),
        P(("gx", "gy", "gz"), None),
    )
    return jax.shard_map(
        shards,
        mesh=mesh,
        in_specs=placed,
        out_specs=(P("gx", "gy", "gz"), P("gx", "gy", "gz")),
        check_vma=False,
    )
```

profile of v0, /device:TPU:1, one launch (start us, length us, event | category | flops | bytes accessed | tf_op | source)
XLA Modules:
  0.0 572.3 jit_solution(1241836847515531308)
XLA Ops:
  2.9 4.6 collective-permute-start.6
  10.3 3.6 collective-permute-start
  15.8 8.8 %fusion.8 = f32[16]{0:T(128)S(1)} fusion(f32[16,16,16,256]{3,2,1,0:T(8,128)} %param.10, f32[16,16,256,1]{2,1,0,3:T(8,128)} %bitcast.289), kind=kOutput, calls=%fused_computation.14 | convolution fusion | flops 12582912 | bytes 4456512 | tf_op jit(solution)/shard_map/dot_general | solution.py:67
  24.8 66.8 %all-reduce.8 = f32[2048]{0:T(1024)S(1)} all-reduce(f32[2048]{0:T(1024)S(1)} %dynamic-update-slice), channel_id=1, replica_groups=mesh['gx'=8,'gy'=4,'gz'=4] {'gx','gy','gz'}, use_global_device_ids=true, to_apply=%add.8 | all-reduce | flops 2048 | bytes 16384
  98.7 4.7 collective-permute-start.8
  105.7 5.1 fusion.2
  110.9 8.1 %copy.37 = f32[5,22,16,256]{2,1,3,0:T(8,128)} copy(f32[5,22,16,256]{3,2,1,0:T(8,128)S(1)} %pad_maximum_fusion.2) | data formatting | bytes 3604480 | tf_op jit(solution)/shard_map/concatenate | solution.py:22
  119.0 9.0 %copy.36 = f32[5,22,3,256]{2,1,3,0:T(8,128)} copy(f32[5,22,3,256]{3,1,2,0:T(8,128)} %collective-permute-done.8) | data formatting | bytes 675840 | tf_op jit(solution)/shard_map/ppermute | solution.py:20
  128.0 9.0 %copy.38 = f32[5,22,3,256]{2,1,3,0:T(8,128)} copy(f32[5,22,3,256]{3,1,2,0:T(8,128)} %collective-permute-done.9) | data formatting | bytes 675840 | tf_op jit(solution)/shard_map/ppermute | solution.py:21
  137.0 16.9 %pad_maximum_fusion = f32[5,22,22,256]{2,1,3,0:T(8,128)S(1)} fusion(f32[5,22,3,256]{2,1,3,0:T(8,128)} %copy.38, f32[5,22,16,256]{2,1,3,0:T(8,128)} %copy.37, f32[5,22,3,256]{2,1,3,0:T(8,128)} %copy.36), kind=kLoop, calls=%fused_computation | loop fusion | flops 1239040 | bytes 4956160 | tf_op jit(solution)/shard_map/concatenate | solution.py:22
  153.8 5.4 copy-done.4
  164.9 4.0 collective-permute-start.4
  170.4 9.2 %copy.40 = f32[5,22,22,256]{3,2,1,0:T(8,128)S(1)} copy(f32[5,22,22,256]{2,1,3,0:T(8,128)} %copy-done.4) | data formatting | bytes 4956160 | tf_op jit(solution)/shard_map/concatenate | solution.py:22
  179.6 3.1 copy.39
  184.6 3.2 pad_maximum_fusion.1
  191.2 3.7 fusion.213
  203.7 4.9 collective-permute-start.12
  213.7 4.3 collective-permute-start.14
  219.3 3.2 collective-permute-done.15
  222.7 4.3 collective-permute-start.16
  232.2 3.9 collective-permute-done.17
  239.0 63.0 %all-reduce.10 = (f32[]{:T(128)}, f32[]{:T(128)}) all-reduce(f32[]{:T(128)} %get-tuple-element.5, f32[]{:T(128)} %get-tuple-element.4), channel_id=1, replica_groups=mesh['gx'=8,'gy'=4,'gz'=4] {'gx','gy','gz'}, use_global_device_ids=true, to_apply=%region_1.2 | all-reduce | flops 2 | bytes 16 | tf_op jit(solution)/shard_map/psum | solution.py:87
  304.5 3.0 collective-permute-start.18
  309.4 8.6 %fusion.11 = f32[16]{0:T(128)S(1)} fusion(f32[16,16,16,256]{3,2,1,0:T(8,128)} %param.10, f32[16,16,256,1]{2,1,0,3:T(8,128)S(1)} %bitcast.285), kind=kOutput, calls=%fused_computation.15 | convolution fusion | flops 12582912 | bytes 4456512 | tf_op jit(solution)/shard_map/dot_general | solution.py:67
  318.3 63.0 %all-reduce.9 = f32[2048]{0:T(1024)S(1)} all-reduce(f32[2048]{0:T(1024)S(1)} %dynamic-update-slice.1), channel_id=1, replica_groups=mesh['gx'=8,'gy'=4,'gz'=4] {'gx','gy','gz'}, use_global_device_ids=true, to_apply=%add.9 | all-reduce | flops 2048 | bytes 16384
  385.6 3.2 collective-permute-done.21
  392.3 6.4 %fusion = f32[1,16,16,256]{3,0,2,1:T(1,128)S(1)} fusion(f32[16,1,1,1]{0,1,3,2:T(1,128)S(1)} %convolution_bitcast_fusion, f32[16,16,256,16]{2,1,0,3:T(8,128)} %bitcast.283), kind=kOutput, calls=%fused_computation.2 | convolution fusion | flops 12582912 | bytes 4456512 | tf_op jit(solution)/shard_map/dot_general | solution.py:73
  407.6 67.1 %psum.30 = f32[]{:T(128)} all-reduce(f32[]{:T(128)} %get-tuple-element.10), channel_id=1, replica_groups=mesh['gx'=8,'gy'=4,'gz'=4] {'gx','gy','gz'}, use_global_device_ids=true, to_apply=%region_5.6 | all-reduce | flops 1 | bytes 8 | tf_op jit(solution)/shard_map/psum | solution.py:87
  488.0 3.2 collective-permute-done.27
  494.6 3.9 collective-permute-done.28
  498.5 3.9 collective-permute-done.29
  506.7 63.2 %psum.31 = f32[]{:T(128)} all-reduce(f32[]{:T(128)} %get-tuple-element.8), channel_id=1, replica_groups=mesh['gx'=8,'gy'=4,'gz'=4] {'gx','gy','gz'}, use_global_device_ids=true, to_apply=%region_7.8 | all-reduce | flops 1 | bytes 8 | tf_op jit(solution)/shard_map/psum | solution.py:117
  (162 shorter events, 92.3 us)
Async XLA Ops:
  1.8 95.9 %copy-start.18 = (f32[1,16,16,256]{3,2,1,0:T(8,128)}, f32[1,16,16,256]{3,2,1,0:T(8,128)S(1)}, u32[]{:S(2)}) copy-start(f32[1,16,16,256]{3,2,1,0:T(8,128)S(1)} %fusion.212) | copy-start | bytes 786436
  2.9 92.8 %collective-permute-start.6 = (f32[5,3,16,256]{3,2,1,0:T(8,128)S(1)}, f32[5,3,16,256]{3,2,1,0:T(8,128)S(1)}, u32[]{:S(2)}, u32[]{:S(2)}) collective-permute-start(f32[5,3,16,256]{3,2,1,0:T(8,128)S(1)} %get-tuple-element.36), channel_id=1, source_target_pairs={{0,16},{16,32},{32,48},{48,64},{64,80},{80,96},{96,112},{1,17},{17... | collective-permute-start | bytes 737288 | tf_op jit(solution)/shard_map/ppermute | solution.py:20
  7.6 88.9 %collective-permute-start.7 = (f32[5,3,16,256]{3,2,1,0:T(8,128)S(1)}, f32[5,3,16,256]{3,2,1,0:T(8,128)}, u32[]{:S(2)}, u32[]{:S(2)}) collective-permute-start(f32[5,3,16,256]{3,2,1,0:T(8,128)S(1)} %get-tuple-element.37), channel_id=1, source_target_pairs={{16,0},{32,16},{48,32},{64,48},{80,64},{96,80},{112,96},{17,1},{33... | collective-permute-start | bytes 737288 | tf_op jit(solution)/shard_map/ppermute | solution.py:21
  10.3 81.6 %collective-permute-start = (f32[2,16,256]{2,1,0:T(8,128)S(1)}, f32[2,16,256]{2,1,0:T(8,128)S(1)}, u32[]{:S(2)}, u32[]{:S(2)}) collective-permute-start(f32[2,16,256]{2,1,0:T(8,128)S(1)} %get-tuple-element.61), channel_id=1, source_target_pairs={{0,16},{16,32},{32,48},{48,64},{64,80},{80,96},{96,112},{1,17},{17... | collective-permute-start | bytes 98312 | tf_op jit(solution)/shard_map/ppermute | solution.py:20
  13.9 78.1 %collective-permute-start.1 = (f32[2,16,256]{2,1,0:T(8,128)S(1)}, f32[2,16,256]{2,1,0:T(8,128)S(1)}, u32[]{:S(2)}, u32[]{:S(2)}) collective-permute-start(f32[2,16,256]{2,1,0:T(8,128)S(1)} %get-tuple-element.60), channel_id=1, source_target_pairs={{16,0},{32,16},{48,32},{64,48},{80,64},{96,80},{112,96},{17,1},{33... | collective-permute-start | bytes 98312 | tf_op jit(solution)/shard_map/ppermute | solution.py:21
  92.0 18.7 %collective-permute-start.2 = (f32[20,2,256]{2,1,0:T(2,128)S(1)}, f32[20,2,256]{2,1,0:T(2,128)S(1)}, u32[]{:S(2)}, u32[]{:S(2)}) collective-permute-start(f32[20,2,256]{2,1,0:T(2,128)S(1)} %get-tuple-element.48), channel_id=1, source_target_pairs={{0,4},{4,8},{8,12},{1,5},{5,9},{9,13},{2,6},{6,10},{10,14},{3,7},{... | collective-permute-start | bytes 122888 | tf_op jit(solution)/shard_map/ppermute | solution.py:20
  94.5 16.3 %collective-permute-start.3 = (f32[20,2,256]{2,1,0:T(2,128)S(1)}, f32[20,2,256]{2,1,0:T(2,128)S(1)}, u32[]{:S(2)}, u32[]{:S(2)}) collective-permute-start(f32[20,2,256]{2,1,0:T(2,128)S(1)} %get-tuple-element.49), channel_id=1, source_target_pairs={{4,0},{8,4},{12,8},{5,1},{9,5},{13,9},{6,2},{10,6},{14,10},{7,3},{... | collective-permute-start | bytes 122888 | tf_op jit(solution)/shard_map/ppermute | solution.py:21
  98.7 20.3 %collective-permute-start.8 = (f32[5,22,3,256]{3,1,2,0:T(8,128)}, f32[5,22,3,256]{3,1,2,0:T(8,128)}, u32[]{:S(2)}, u32[]{:S(2)}) collective-permute-start(f32[5,22,3,256]{3,1,2,0:T(8,128)} %copy.55), channel_id=1, source_target_pairs={{0,4},{4,8},{8,12},{1,5},{5,9},{9,13},{2,6},{6,10},{10,14},{3,7},{... | collective-permute-start | bytes 1013768 | tf_op jit(solution)/shard_map/ppermute | solution.py:20
  104.3 23.8 %collective-permute-start.9 = (f32[5,22,3,256]{3,1,2,0:T(8,128)}, f32[5,22,3,256]{3,1,2,0:T(8,128)}, u32[]{:S(2)}, u32[]{:S(2)}) collective-permute-start(f32[5,22,3,256]{3,1,2,0:T(8,128)} %copy.56), channel_id=1, source_target_pairs={{4,0},{8,4},{12,8},{5,1},{9,5},{13,9},{6,2},{10,6},{14,10},{7,3},{... | collective-permute-start | bytes 1013768 | tf_op jit(solution)/shard_map/ppermute | solution.py:21
  160.0 19.6 %collective-permute-start.10 = (f32[5,22,22,3]{2,1,3,0:T(8,128)}, f32[5,22,22,3]{2,1,3,0:T(8,128)}, u32[]{:S(2)}, u32[]{:S(2)}) collective-permute-start(f32[5,22,22,3]{2,1,3,0:T(8,128)} %get-tuple-element.30), channel_id=1, source_target_pairs={{0,1},{1,2},{2,3},{4,5},{5,6},{6,7},{8,9},{9,10},{10,11},{12,13},{... | collective-permute-start | bytes 87128 | tf_op jit(solution)/shard_map/ppermute | solution.py:20
  162.7 20.0 %collective-permute-start.11 = (f32[5,22,22,3]{2,1,3,0:T(8,128)}, f32[5,22,22,3]{2,1,3,0:T(8,128)S(1)}, u32[]{:S(2)}, u32[]{:S(2)}) collective-permute-start(f32[5,22,22,3]{2,1,3,0:T(8,128)} %get-tuple-element.31), channel_id=1, source_target_pairs={{1,0},{2,1},{3,2},{5,4},{6,5},{7,6},{9,8},{10,9},{11,10},{13,12},{... | collective-permute-start | bytes 87128 | tf_op jit(solution)/shard_map/ppermute | solution.py:21
  164.9 25.7 %collective-permute-start.4 = (f32[20,20,2]{2,1,0:T(8,128)}, f32[20,20,2]{2,1,0:T(8,128)S(1)}, u32[]{:S(2)}, u32[]{:S(2)}) collective-permute-start(f32[20,20,2]{2,1,0:T(8,128)} %get-tuple-element.40), channel_id=1, source_target_pairs={{0,1},{1,2},{2,3},{4,5},{5,6},{6,7},{8,9},{9,10},{10,11},{12,13},{... | collective-permute-start | bytes 9608 | tf_op jit(solution)/shard_map/ppermute | solution.py:20
  168.9 22.4 %collective-permute-start.5 = (f32[20,20,2]{2,1,0:T(8,128)}, f32[20,20,2]{2,1,0:T(8,128)}, u32[]{:S(2)}, u32[]{:S(2)}) collective-permute-start(f32[20,20,2]{2,1,0:T(8,128)} %get-tuple-element.41), channel_id=1, source_target_pairs={{1,0},{2,1},{3,2},{5,4},{6,5},{7,6},{9,8},{10,9},{11,10},{13,12},{... | collective-permute-start | bytes 9608 | tf_op jit(solution)/shard_map/ppermute | solution.py:21
  203.7 7.3 %collective-permute-start.12 = (f32[1,16,256]{2,1,0:T(8,128)S(1)}, f32[1,16,256]{2,1,0:T(8,128)S(1)}, u32[]{:S(2)}, u32[]{:S(2)}) collective-permute-start(f32[1,16,256]{2,1,0:T(8,128)S(1)} %get-tuple-element.58), channel_id=1, source_target_pairs={{0,16},{16,32},{32,48},{48,64},{64,80},{80,96},{96,112},{1,17},{17... | collective-permute-start | bytes 49160 | tf_op jit(solution)/shard_map/ppermute | solution.py:20
  208.6 5.1 collective-permute-start.13
  213.7 5.6 collective-permute-start.14
  218.0 4.5 collective-permute-start.15
  222.7 9.5 %collective-permute-start.16 = (f32[18,18,1]{2,1,0:T(8,128)S(1)}, f32[18,18,1]{2,1,0:T(8,128)S(1)}, u32[]{:S(2)}, u32[]{:S(2)}) collective-permute-start(f32[18,18,1]{2,1,0:T(8,128)S(1)} %get-tuple-element.44), channel_id=1, source_target_pairs={{0,1},{1,2},{2,3},{4,5},{5,6},{6,7},{8,9},{9,10},{10,11},{12,13},{... | collective-permute-start | bytes 3896 | tf_op jit(solution)/shard_map/ppermute | solution.py:20
  227.0 9.1 %collective-permute-start.17 = (f32[18,18,1]{2,1,0:T(8,128)S(1)}, f32[18,18,1]{2,1,0:T(8,128)S(1)}, u32[]{:S(2)}, u32[]{:S(2)}) collective-permute-start(f32[18,18,1]{2,1,0:T(8,128)S(1)} %get-tuple-element.45), channel_id=1, source_target_pairs={{1,0},{2,1},{3,2},{5,4},{6,5},{7,6},{9,8},{10,9},{11,10},{13,12},{... | collective-permute-start | bytes 3896 | tf_op jit(solution)/shard_map/ppermute | solution.py:21
  304.5 76.9 %collective-permute-start.18 = (f32[2,16,256]{2,1,0:T(8,128)S(1)}, f32[2,16,256]{2,1,0:T(8,128)S(1)}, u32[]{:S(2)}, u32[]{:S(2)}) collective-permute-start(f32[2,16,256]{2,1,0:T(8,128)S(1)} %get-tuple-element.56), channel_id=1, source_target_pairs={{0,16},{16,32},{32,48},{48,64},{64,80},{80,96},{96,112},{1,17},{17... | collective-permute-start | bytes 98312 | tf_op jit(solution)/shard_map/ppermute | solution.py:20
  307.5 73.8 %collective-permute-start.19 = (f32[2,16,256]{2,1,0:T(8,128)S(1)}, f32[2,16,256]{2,1,0:T(8,128)S(1)}, u32[]{:S(2)}, u32[]{:S(2)}) collective-permute-start(f32[2,16,256]{2,1,0:T(8,128)S(1)} %get-tuple-element.57), channel_id=1, source_target_pairs={{16,0},{32,16},{48,32},{64,48},{80,64},{96,80},{112,96},{17,1},{33... | collective-permute-start | bytes 98312 | tf_op jit(solution)/shard_map/ppermute | solution.py:21
  381.4 4.2 collective-permute-start.20
  384.1 4.7 collective-permute-start.21
  389.0 9.7 %collective-permute-start.22 = (f32[20,20,2]{2,1,0:T(8,128)S(1)}, f32[20,20,2]{2,1,0:T(8,128)S(1)}, u32[]{:S(2)}, u32[]{:S(2)}) collective-permute-start(f32[20,20,2]{2,1,0:T(8,128)S(1)} %get-tuple-element.38), channel_id=1, source_target_pairs={{0,1},{1,2},{2,3},{4,5},{5,6},{6,7},{8,9},{9,10},{10,11},{12,13},{... | collective-permute-start | bytes 9608 | tf_op jit(solution)/shard_map/ppermute | solution.py:20
  390.8 7.9 %collective-permute-start.23 = (f32[20,20,2]{2,1,0:T(8,128)S(1)}, f32[20,20,2]{2,1,0:T(8,128)S(1)}, u32[]{:S(2)}, u32[]{:S(2)}) collective-permute-start(f32[20,20,2]{2,1,0:T(8,128)S(1)} %get-tuple-element.39), channel_id=1, source_target_pairs={{1,0},{2,1},{3,2},{5,4},{6,5},{7,6},{9,8},{10,9},{11,10},{13,12},{... | collective-permute-start | bytes 9608 | tf_op jit(solution)/shard_map/ppermute | solution.py:21
  405.0 99.2 %copy-start.9 = (f32[3,16,16,256]{3,2,1,0:T(8,128)S(1)}, f32[3,16,16,256]{3,2,1,0:T(8,128)}, u32[]{:S(2)}) copy-start(f32[3,16,16,256]{3,2,1,0:T(8,128)} %param.7) | copy-start | bytes 2359300
  476.9 4.3 collective-permute-start.24
  479.1 5.1 collective-permute-start.25
  484.2 3.8 collective-permute-start.26
  486.6 4.6 collective-permute-start.27
  491.4 7.1 %collective-permute-start.28 = (f32[18,18,1]{2,1,0:T(8,128)S(1)}, f32[18,18,1]{2,1,0:T(8,128)S(1)}, u32[]{:S(2)}, u32[]{:S(2)}) collective-permute-start(f32[18,18,1]{2,1,0:T(8,128)S(1)} %get-tuple-element.42), channel_id=1, source_target_pairs={{0,1},{1,2},{2,3},{4,5},{5,6},{6,7},{8,9},{9,10},{10,11},{12,13},{... | collective-permute-start | bytes 3896 | tf_op jit(solution)/shard_map/ppermute | solution.py:20
  493.3 9.1 %collective-permute-start.29 = (f32[18,18,1]{2,1,0:T(8,128)S(1)}, f32[18,18,1]{2,1,0:T(8,128)S(1)}, u32[]{:S(2)}, u32[]{:S(2)}) collective-permute-start(f32[18,18,1]{2,1,0:T(8,128)S(1)} %get-tuple-element.43), channel_id=1, source_target_pairs={{1,0},{2,1},{3,2},{5,4},{6,5},{7,6},{9,8},{10,9},{11,10},{13,12},{... | collective-permute-start | bytes 3896 | tf_op jit(solution)/shard_map/ppermute | solution.py:21
  (30 other events, 940.6 us)
where the time goes:
time: 581 us; the launch traced here: 572 us
  blocking collectives  323 us (56%)
  starting transfers between devices  73.3 us (13%)
  local copies, waits for them, and re-layouts  55.9 us (10%)
  other arithmetic  55.2 us (10%)
  waiting for transfers between devices  29.9 us (5%)
  matrix products  29.2 us (5%)
    psum x2, blocking collectives, norm_sum(): return lax.psum(value, ('gx', 'gy', 'gz'))  130 us
    unnamed x2, blocking collectives  130 us
    psum x1, blocking collectives, shards(): curvature = lax.psum(local_curve, ('gx', 'gy', 'gz'))  63.2 us
    ppermute x15, starting transfers between devices, padded(): before = lax.ppermute(last, axis, up)  49.5 us
    ppermute x15, starting transfers between devices, padded(): after = lax.ppermute(leading, axis, down)  23.7 us
    ppermute x15, waiting for transfers between devices, padded(): after = lax.ppermute(leading, axis, down)  23.2 us
    concatenate x7, other arithmetic, padded(): value = jnp.concatenate([before, value, after], axis=dim)  21.5 us
    dot_general x2, matrix products, project(): jnp.dot(basis.reshape(basis.shape[0], -1), field.reshape(-1), precision=l...  17.4 us
  transfers between devices with their start and end apart: 30, of which 9 were waited for; matrix products, arithmetic and copies ran while one was open for 13% of the time, Pallas kernels for 0%

commit v1 on v0

--- a/solution.py
+++ b/solution.py
@@ -75,19 +75,34 @@
     ).reshape(field.shape)
 
 
-def gather_coarse(values):
-    return lax.all_gather(values, ("gx", "gy", "gz"), axis=0, tiled=True)
+LANES = 128
 
 
 def residual_rim(field):
     return padded(field, (("gx", 0), ("gy", 1), ("gz", 2)), 2)
 
 
-def norm_sum(value):
-    return lax.psum(value, ("gx", "gy", "gz"))
+def gather_rows(row):
+    return lax.all_gather(row, ("gx", "gy", "gz"), axis=0, tiled=True)
+
+
+def pack(coarse, scalars):
+    vecs = coarse.shape[0]
+    row = jnp.zeros((LANES,), jnp.float32)
+    row = row.at[:vecs].set(coarse)
+    if scalars:
+        row = row.at[vecs:vecs + len(scalars)].set(jnp.stack(scalars))
+    return row[None]
+
+
+def unpack(rows, vecs, count):
+    coarse = rows[:, :vecs].reshape(-1)
+    sums = jnp.sum(rows[:, vecs:vecs + count], axis=0)
+    return coarse, [sums[i] for i in range(count)]
 
 
 def shards(right_side, conductance, storage, dirichlet, basis, coarse_inverse):
+    vecs = basis.shape[0]
     free = 1.0 - dirichlet.astype(jnp.float32)
     stacked = jnp.concatenate([conductance, storage[None], free[None]], axis=0)
     wide = padded(stacked, (("gx", 1), ("gy", 2), ("gz", 3)), 3)
@@ -102,32 +117,43 @@
     def schwarz(rhs_box):
         return jacobi(rhs_box, box_cond, box_diag, storage_box, free_box)[2:-2, 2:-2, 2:-2]
 
-    solution = jnp.zeros_like(right_side)
-    residual = right_side
-    rhs_box = residual_rim(residual)
-    coarse_now = project(basis, residual)
-    weights = jnp.dot(coarse_inverse, gather_coarse(coarse_now), precision=lax.Precision.HIGHEST)
-    precond = schwarz(rhs_box) + expand(basis, weights, residual)
-    norm_now = norm_sum(jnp.sum(residual * precond))
-    direction = precond
-    for step in range(ITERS):
-        near_dir = padded(direction, (("gx", 0), ("gy", 1), ("gz", 2)), 1)
-        image = stencil(free_face * near_dir, cond_face, direction, storage, free)
-        local_curve = jnp.sum(direction * image)
-        curvature = lax.psum(local_curve, ("gx", "gy", "gz"))
-        alpha = norm_now / curvature
-        solution = solution + alpha * direction
-        residual = residual - alpha * image
-        if step + 1 < ITERS:
-            rhs_box = residual_rim(residual)
-            coarse_now = project(basis, residual)
-            gathered = gather_coarse(coarse_now)
-            weights = jnp.dot(coarse_inverse, gathered, precision=lax.Precision.HIGHEST)
-            precond = schwarz(rhs_box) + expand(basis, weights, residual)
-            norm_next = norm_sum(jnp.sum(residual * precond))
-            direction = precond + norm_next / norm_now * direction
-            norm_now = norm_next
-    return (solution, residual)
+    def apply(field):
+        near = padded(field, (("gx", 0), ("gy", 1), ("gz", 2)), 1)
+        return stencil(free_face * near, cond_face, field, storage, free)
+
+    def precondition(residual, coarse_all):
+        weights = jnp.dot(coarse_inverse, coarse_all, precision=lax.Precision.HIGHEST)
+        return schwarz(residual_rim(residual)) + expand(basis, weights, residual)
+
+    residual0 = right_side
+    coarse0 = project(basis, residual0)
+    coarse0_all, _ = unpack(gather_rows(pack(coarse0, [])), vecs, 0)
+    z0 = precondition(residual0, coarse0_all)
+    image0 = apply(z0)
+    coarse_img = project(basis, image0)
+    rows = gather_rows(pack(coarse_img, [jnp.sum(residual0 * z0), jnp.sum(z0 * image0)]))
+    coarse_img_all, (rz0, curve0) = unpack(rows, vecs, 2)
+    alpha0 = rz0 / curve0
+    solution1 = alpha0 * z0
+    residual1 = residual0 - alpha0 * image0
+    coarse1_all = coarse0_all - alpha0 * coarse_img_all
+    z1 = precondition(residual1, coarse1_all)
+    image_z1 = apply(z1)
+    local = [
+        jnp.sum(residual1 * z1),
+        jnp.sum(z1 * image_z1),
+        jnp.sum(z1 * image0),
+        jnp.sum(z0 * image_z1),
+    ]
+    _, (rz1, zz, cross_a, cross_b) = unpack(gather_rows(pack(jnp.zeros((0,), jnp.float32), local)), 0, 4)
+    beta = rz1 / rz0
+    direction1 = z1 + beta * z0
+    image1 = image_z1 + beta * image0
+    curve1 = zz + beta * (cross_a + cross_b) + beta * beta * curve0
+    alpha1 = rz1 / curve1
+    solution2 = solution1 + alpha1 * direction1
+    residual2 = residual1 - alpha1 * image1
+    return (solution2, residual2)
 
 
 def solution(mesh):

time: 581 us -> 401 us (0.69)
  blocking collectives: 323 us -> 134 us
    psum x3 -> x0, blocking collectives: 193 us -> none  [the longest x2 130 us: norm_sum(): return lax.psum(value, ('gx', 'gy', 'gz'))]
    all_gather x0 -> x3, blocking collectives: none -> 134 us  [gather_rows(): return lax.all_gather(row, ('gx', 'gy', 'gz'), axis=0, tiled=True)]
    unnamed x2 -> x0, blocking collectives: 130 us -> none
  transfers between devices with their start and end apart: 30 -> 30, of which waited for: 9 -> 11; matrix products, arithmetic and copies ran while one was open for 13% -> 16% of each run, Pallas kernels for 0% -> 0%
where the time goes in v1:
time: 401 us; the launch traced here: 393 us
  blocking collectives  134 us (33%)
  starting transfers between devices  75.1 us (19%)
  local copies, waits for them, and re-layouts  58.7 us (15%)
  other arithmetic  58 us (14%)
  waiting for transfers between devices  32.5 us (8%)
  matrix products  27.6 us (7%)
  between operations  7.57 us (2%)
    all_gather x3, blocking collectives, gather_rows(): return lax.all_gather(row, ('gx', 'gy', 'gz'), axis=0, tiled=True)  134 us
    ppermute x15, starting transfers between devices, padded(): before = lax.ppermute(last, axis, up)  50.3 us
    ppermute x15, waiting for transfers between devices, padded(): after = lax.ppermute(leading, axis, down)  27.8 us
    ppermute x15, starting transfers between devices, padded(): after = lax.ppermute(leading, axis, down)  24.8 us
    concatenate x7, other arithmetic, padded(): value = jnp.concatenate([before, value, after], axis=dim)  22.5 us
    concatenate x3, local copies, waits for them, and re-layouts, padded(): value = jnp.concatenate([before, value, after], axis=dim)  17.4 us
    dot_general x2, matrix products, project(): jnp.dot(basis.reshape(basis.shape[0], -1), field.reshape(-1), precision=l...  15.8 us
    mul x7, other arithmetic, jacobi(): free_box * guess  12.6 us
  transfers between devices with their start and end apart: 30, of which 11 were waited for; matrix products, arithmetic and copies ran while one was open for 16% of the time, Pallas kernels for 0%

profile of v1, /device:TPU:1, one launch (start us, length us, event | category | flops | bytes accessed | tf_op | source)
XLA Modules:
  0.0 393.4 jit_solution(8084429038879911212)
XLA Ops:
  3.0 4.6 %collective-permute-start = (f32[5,3,16,256]{3,2,1,0:T(8,128)S(1)}, f32[5,3,16,256]{3,2,1,0:T(8,128)S(1)}, u32[]{:S(2)}, u32[]{:S(2)}) collective-permute-start(f32[5,3,16,256]{3,2,1,0:T(8,128)S(1)} %get-tuple-element.83), channel_id=1, source_target_pairs={{0,16},{16,32},{32,48},{48,64},{64,80},{80,96},{96,112},{1,17},{17... | collective-permute-start | bytes 737288 | tf_op jit(solution)/shard_map/ppermute | solution.py:20
  10.3 3.6 collective-permute-start.6
  15.8 8.8 %fusion.8 = f32[1,16]{1,0:T(1,128)S(1)} fusion(f32[16,16,16,256]{3,2,1,0:T(8,128)} %param.18, f32[16,16,256,1]{2,1,0,3:T(8,128)} %bitcast.314), kind=kOutput, calls=%fused_computation.14 | convolution fusion | flops 12582912 | bytes 4456512 | tf_op jit(solution)/shard_map/dot_general | solution.py:67
  24.6 46.9 %all-gather = f32[128,1,128]{2,1,0:T(1,128)S(1)} all-gather(f32[1,1,128]{2,1,0:T(1,128)S(1)} %pad_bitcast_fusion.2), channel_id=1, replica_groups=mesh['gx'=8,'gy'=4,'gz'=4] {'gx','gy','gz'}, dimensions={0}, use_global_device_ids=true | all-gather | bytes 66048 | tf_op jit(solution)/shard_map/all_gather | solution.py:86
  78.3 4.0 %collective-permute-start.2 = (f32[5,22,3,256]{3,1,2,0:T(8,128)}, f32[5,22,3,256]{3,1,2,0:T(8,128)S(1)}, u32[]{:S(2)}, u32[]{:S(2)}) collective-permute-start(f32[5,22,3,256]{3,1,2,0:T(8,128)} %copy.55), channel_id=1, source_target_pairs={{0,4},{4,8},{8,12},{1,5},{5,9},{9,13},{2,6},{6,10},{10,14},{3,7},{... | collective-permute-start | bytes 1013768 | tf_op jit(solution)/shard_map/ppermute | solution.py:20
  84.5 5.1 %fusion.2 = f32[1,16,16,256]{3,0,2,1:T(1,128)} fusion(f32[16,1,1,1]{0,1,3,2:T(1,128)S(1)} %convolution_bitcast_fusion.1, f32[16,16,256,16]{2,1,0,3:T(8,128)S(1)} %bitcast.309), kind=kOutput, calls=%fused_computation.4 | convolution fusion | flops 12582912 | bytes 4456512 | tf_op jit(solution)/shard_map/dot_general | solution.py:73
  90.9 8.2 %copy.37 = f32[5,22,16,256]{2,1,3,0:T(8,128)} copy(f32[5,22,16,256]{3,2,1,0:T(8,128)S(1)} %pad_maximum_fusion.2) | data formatting | bytes 3604480 | tf_op jit(solution)/shard_map/concatenate | solution.py:22
  99.1 8.1 %copy.36 = f32[5,22,3,256]{2,1,3,0:T(8,128)} copy(f32[5,22,3,256]{3,1,2,0:T(8,128)S(1)} %collective-permute-done.2) | data formatting | bytes 675840 | tf_op jit(solution)/shard_map/ppermute | solution.py:20
  107.2 8.8 %copy.38 = f32[5,22,3,256]{2,1,3,0:T(8,128)} copy(f32[5,22,3,256]{3,1,2,0:T(8,128)} %collective-permute-done.3) | data formatting | bytes 675840 | tf_op jit(solution)/shard_map/ppermute | solution.py:21
  116.1 16.9 %pad_maximum_fusion = f32[5,22,22,256]{2,1,3,0:T(8,128)S(1)} fusion(f32[5,22,3,256]{2,1,3,0:T(8,128)} %copy.38, f32[5,22,16,256]{2,1,3,0:T(8,128)} %copy.37, f32[5,22,3,256]{2,1,3,0:T(8,128)} %copy.36), kind=kLoop, calls=%fused_computation | loop fusion | flops 1239040 | bytes 4956160 | tf_op jit(solution)/shard_map/concatenate | solution.py:22
  132.9 5.4 %copy-done.5 = f32[5,22,22,256]{2,1,3,0:T(8,128)} copy-done((f32[5,22,22,256]{2,1,3,0:T(8,128)}, f32[5,22,22,256]{2,1,3,0:T(8,128)S(1)}, u32[]{:S(2)}) %copy-start.5) | copy-done | bytes 2478104
  139.1 3.5 collective-permute-start.4
  144.7 4.0 %collective-permute-start.10 = (f32[20,20,2]{2,1,0:T(8,128)}, f32[20,20,2]{2,1,0:T(8,128)S(1)}, u32[]{:S(2)}, u32[]{:S(2)}) collective-permute-start(f32[20,20,2]{2,1,0:T(8,128)} %get-tuple-element.87), channel_id=1, source_target_pairs={{0,1},{1,2},{2,3},{4,5},{5,6},{6,7},{8,9},{9,10},{10,11},{12,13},{... | collective-permute-start | bytes 9608 | tf_op jit(solution)/shard_map/ppermute | solution.py:20
  150.2 9.2 %copy.40 = f32[5,22,22,256]{3,2,1,0:T(8,128)S(1)} copy(f32[5,22,22,256]{2,1,3,0:T(8,128)} %copy-done.5) | data formatting | bytes 4956160 | tf_op jit(solution)/shard_map/concatenate | solution.py:22
  159.4 3.1 copy.39
  165.3 3.2 pad_maximum_fusion.1
  170.0 3.8 fusion.213
  187.7 4.3 %collective-permute-start.14 = (f32[18,1,256]{2,1,0:T(1,128)S(1)}, f32[18,1,256]{2,1,0:T(1,128)S(1)}, u32[]{:S(2)}, u32[]{:S(2)}) collective-permute-start(f32[18,1,256]{2,1,0:T(1,128)S(1)} %get-tuple-element.99), channel_id=1, source_target_pairs={{0,4},{4,8},{8,12},{1,5},{5,9},{9,13},{2,6},{6,10},{10,14},{3,7},{... | collective-permute-start | bytes 55304 | tf_op jit(solution)/shard_map/ppermute | solution.py:20
  193.7 3.2 collective-permute-done.15
  197.7 5.0 %collective-permute-start.16 = (f32[18,18,1]{2,1,0:T(8,128)}, f32[18,18,1]{2,1,0:T(8,128)}, u32[]{:S(2)}, u32[]{:S(2)}) collective-permute-start(f32[18,18,1]{2,1,0:T(8,128)} %get-tuple-element.91), channel_id=1, source_target_pairs={{0,1},{1,2},{2,3},{4,5},{5,6},{6,7},{8,9},{9,10},{10,11},{12,13},{... | collective-permute-start | bytes 3896 | tf_op jit(solution)/shard_map/ppermute | solution.py:20
  206.8 4.5 %collective-permute-done.17 = f32[18,18,1]{2,1,0:T(8,128)} collective-permute-done((f32[18,18,1]{2,1,0:T(8,128)}, f32[18,18,1]{2,1,0:T(8,128)}, u32[]{:S(2)}, u32[]{:S(2)}) %collective-permute-start.17) | collective-permute-done | bytes 1328 | tf_op jit(solution)/shard_map/ppermute | solution.py:21
  213.2 3.8 multiply_reduce_fusion.5
  217.0 7.0 %fusion.11 = f32[16]{0:T(128)S(1)} fusion(f32[16,16,16,256]{3,2,1,0:T(8,128)S(1)} %copy-done.4, f32[16,16,256,1]{2,1,0,3:T(8,128)S(1)} %bitcast.313), kind=kOutput, calls=%fused_computation.15 | convolution fusion | flops 12582912 | bytes 4456512 | tf_op jit(solution)/shard_map/dot_general | solution.py:67
  225.6 44.1 %all-gather.1 = f32[128,1,128]{2,1,0:T(1,128)S(1)} all-gather(f32[1,1,128]{2,1,0:T(1,128)S(1)} %scatter.24), channel_id=1, replica_groups=mesh['gx'=8,'gy'=4,'gz'=4] {'gx','gy','gz'}, dimensions={0}, use_global_device_ids=true | all-gather | bytes 66048 | tf_op jit(solution)/shard_map/all_gather | solution.py:86
  286.5 3.2 collective-permute-done.21
  295.4 6.4 %fusion = f32[1,16,16,256]{3,0,2,1:T(1,128)S(1)} fusion(f32[16,1,1,1]{0,1,3,2:T(1,128)S(1)} %convolution_bitcast_fusion, f32[16,16,256,16]{2,1,0,3:T(8,128)} %bitcast.308), kind=kOutput, calls=%fused_computation.2 | convolution fusion | flops 12582912 | bytes 4456512 | tf_op jit(solution)/shard_map/dot_general | solution.py:73
  316.0 3.1 collective-permute-done.25
  323.2 3.2 collective-permute-done.27
  326.6 4.1 %collective-permute-start.28 = (f32[18,18,1]{2,1,0:T(8,128)S(1)}, f32[18,18,1]{2,1,0:T(8,128)S(1)}, u32[]{:S(2)}, u32[]{:S(2)}) collective-permute-start(f32[18,18,1]{2,1,0:T(8,128)S(1)} %get-tuple-element.89), channel_id=1, source_target_pairs={{0,1},{1,2},{2,3},{4,5},{5,6},{6,7},{8,9},{9,10},{10,11},{12,13},{... | collective-permute-start | bytes 3896 | tf_op jit(solution)/shard_map/ppermute | solution.py:20
  332.1 3.9 collective-permute-done.28
  336.0 3.9 collective-permute-done.29
  344.4 42.8 %all-gather.2 = f32[128,1,128]{2,1,0:T(1,128)S(1)} all-gather(f32[1,1,128]{2,1,0:T(1,128)S(1)} %pad_bitcast_fusion), channel_id=1, replica_groups=mesh['gx'=8,'gy'=4,'gz'=4] {'gx','gy','gz'}, dimensions={0}, use_global_device_ids=true | all-gather | bytes 66048 | tf_op jit(solution)/shard_map/all_gather | solution.py:86
  (180 shorter events, 96.1 us)
Async XLA Ops:
  0.6 75.4 %copy-start.15 = (f32[16,16,256]{2,1,0:T(8,128)S(1)}, f32[16,16,256]{2,1,0:T(8,128)}, u32[]{:S(2)}) copy-start(f32[16,16,256]{2,1,0:T(8,128)} %param.16) | copy-start | bytes 786436
  1.8 75.5 %copy-start.20 = (f32[1,16,16,256]{3,2,1,0:T(8,128)}, f32[1,16,16,256]{3,2,1,0:T(8,128)S(1)}, u32[]{:S(2)}) copy-start(f32[1,16,16,256]{3,2,1,0:T(8,128)S(1)} %fusion.212) | copy-start | bytes 786436
  3.0 73.1 %collective-permute-start = (f32[5,3,16,256]{3,2,1,0:T(8,128)S(1)}, f32[5,3,16,256]{3,2,1,0:T(8,128)S(1)}, u32[]{:S(2)}, u32[]{:S(2)}) collective-permute-start(f32[5,3,16,256]{3,2,1,0:T(8,128)S(1)} %get-tuple-element.83), channel_id=1, source_target_pairs={{0,16},{16,32},{32,48},{48,64},{64,80},{80,96},{96,112},{1,17},{17... | collective-permute-start | bytes 737288 | tf_op jit(solution)/shard_map/ppermute | solution.py:20
  7.6 68.5 %collective-permute-start.1 = (f32[5,3,16,256]{3,2,1,0:T(8,128)S(1)}, f32[5,3,16,256]{3,2,1,0:T(8,128)}, u32[]{:S(2)}, u32[]{:S(2)}) collective-permute-start(f32[5,3,16,256]{3,2,1,0:T(8,128)S(1)} %get-tuple-element.84), channel_id=1, source_target_pairs={{16,0},{32,16},{48,32},{64,48},{80,64},{96,80},{112,96},{17,1},{33... | collective-permute-start | bytes 737288 | tf_op jit(solution)/shard_map/ppermute | solution.py:21
  10.3 61.5 %collective-permute-start.6 = (f32[2,16,256]{2,1,0:T(8,128)S(1)}, f32[2,16,256]{2,1,0:T(8,128)S(1)}, u32[]{:S(2)}, u32[]{:S(2)}) collective-permute-start(f32[2,16,256]{2,1,0:T(8,128)S(1)} %get-tuple-element.108), channel_id=1, source_target_pairs={{0,16},{16,32},{32,48},{48,64},{64,80},{80,96},{96,112},{1,17},{17... | collective-permute-start | bytes 98312 | tf_op jit(solution)/shard_map/ppermute | solution.py:20
  13.9 58.0 %collective-permute-start.7 = (f32[2,16,256]{2,1,0:T(8,128)S(1)}, f32[2,16,256]{2,1,0:T(8,128)S(1)}, u32[]{:S(2)}, u32[]{:S(2)}) collective-permute-start(f32[2,16,256]{2,1,0:T(8,128)S(1)} %get-tuple-element.107), channel_id=1, source_target_pairs={{16,0},{32,16},{48,32},{64,48},{80,64},{96,80},{112,96},{17,1},{33... | collective-permute-start | bytes 98312 | tf_op jit(solution)/shard_map/ppermute | solution.py:21
  72.0 17.6 %collective-permute-start.8 = (f32[20,2,256]{2,1,0:T(2,128)S(1)}, f32[20,2,256]{2,1,0:T(2,128)S(1)}, u32[]{:S(2)}, u32[]{:S(2)}) collective-permute-start(f32[20,2,256]{2,1,0:T(2,128)S(1)} %get-tuple-element.95), channel_id=1, source_target_pairs={{0,4},{4,8},{8,12},{1,5},{5,9},{9,13},{2,6},{6,10},{10,14},{3,7},{... | collective-permute-start | bytes 122888 | tf_op jit(solution)/shard_map/ppermute | solution.py:20
  74.7 14.9 %collective-permute-start.9 = (f32[20,2,256]{2,1,0:T(2,128)S(1)}, f32[20,2,256]{2,1,0:T(2,128)S(1)}, u32[]{:S(2)}, u32[]{:S(2)}) collective-permute-start(f32[20,2,256]{2,1,0:T(2,128)S(1)} %get-tuple-element.96), channel_id=1, source_target_pairs={{4,0},{8,4},{12,8},{5,1},{9,5},{13,9},{6,2},{10,6},{14,10},{7,3},{... | collective-permute-start | bytes 122888 | tf_op jit(solution)/shard_map/ppermute | solution.py:21
  78.3 20.8 %collective-permute-start.2 = (f32[5,22,3,256]{3,1,2,0:T(8,128)}, f32[5,22,3,256]{3,1,2,0:T(8,128)S(1)}, u32[]{:S(2)}, u32[]{:S(2)}) collective-permute-start(f32[5,22,3,256]{3,1,2,0:T(8,128)} %copy.55), channel_id=1, source_target_pairs={{0,4},{4,8},{8,12},{1,5},{5,9},{9,13},{2,6},{6,10},{10,14},{3,7},{... | collective-permute-start | bytes 1013768 | tf_op jit(solution)/shard_map/ppermute | solution.py:20
  83.1 24.2 %collective-permute-start.3 = (f32[5,22,3,256]{3,1,2,0:T(8,128)}, f32[5,22,3,256]{3,1,2,0:T(8,128)}, u32[]{:S(2)}, u32[]{:S(2)}) collective-permute-start(f32[5,22,3,256]{3,1,2,0:T(8,128)} %copy.56), channel_id=1, source_target_pairs={{4,0},{8,4},{12,8},{5,1},{9,5},{13,9},{6,2},{10,6},{14,10},{7,3},{... | collective-permute-start | bytes 1013768 | tf_op jit(solution)/shard_map/ppermute | solution.py:21
  139.1 20.3 %collective-permute-start.4 = (f32[5,22,22,3]{2,1,3,0:T(8,128)}, f32[5,22,22,3]{2,1,3,0:T(8,128)}, u32[]{:S(2)}, u32[]{:S(2)}) collective-permute-start(f32[5,22,22,3]{2,1,3,0:T(8,128)} %get-tuple-element.77), channel_id=1, source_target_pairs={{0,1},{1,2},{2,3},{4,5},{5,6},{6,7},{8,9},{9,10},{10,11},{12,13},{... | collective-permute-start | bytes 87128 | tf_op jit(solution)/shard_map/ppermute | solution.py:20
  142.6 20.0 %collective-permute-start.5 = (f32[5,22,22,3]{2,1,3,0:T(8,128)}, f32[5,22,22,3]{2,1,3,0:T(8,128)}, u32[]{:S(2)}, u32[]{:S(2)}) collective-permute-start(f32[5,22,22,3]{2,1,3,0:T(8,128)} %get-tuple-element.78), channel_id=1, source_target_pairs={{1,0},{2,1},{3,2},{5,4},{6,5},{7,6},{9,8},{10,9},{11,10},{13,12},{... | collective-permute-start | bytes 87128 | tf_op jit(solution)/shard_map/ppermute | solution.py:21
  144.7 25.3 %collective-permute-start.10 = (f32[20,20,2]{2,1,0:T(8,128)}, f32[20,20,2]{2,1,0:T(8,128)S(1)}, u32[]{:S(2)}, u32[]{:S(2)}) collective-permute-start(f32[20,20,2]{2,1,0:T(8,128)} %get-tuple-element.87), channel_id=1, source_target_pairs={{0,1},{1,2},{2,3},{4,5},{5,6},{6,7},{8,9},{9,10},{10,11},{12,13},{... | collective-permute-start | bytes 9608 | tf_op jit(solution)/shard_map/ppermute | solution.py:20
  148.7 21.3 %collective-permute-start.11 = (f32[20,20,2]{2,1,0:T(8,128)S(1)}, f32[20,20,2]{2,1,0:T(8,128)}, u32[]{:S(2)}, u32[]{:S(2)}) collective-permute-start(f32[20,20,2]{2,1,0:T(8,128)S(1)} %get-tuple-element.88), channel_id=1, source_target_pairs={{1,0},{2,1},{3,2},{5,4},{6,5},{7,6},{9,8},{10,9},{11,10},{13,12},{... | collective-permute-start | bytes 9608 | tf_op jit(solution)/shard_map/ppermute | solution.py:21
  180.5 4.9 %collective-permute-start.12 = (f32[1,16,256]{2,1,0:T(8,128)S(1)}, f32[1,16,256]{2,1,0:T(8,128)S(1)}, u32[]{:S(2)}, u32[]{:S(2)}) collective-permute-start(f32[1,16,256]{2,1,0:T(8,128)S(1)} %get-tuple-element.105), channel_id=1, source_target_pairs={{0,16},{16,32},{32,48},{48,64},{64,80},{80,96},{96,112},{1,17},{17... | collective-permute-start | bytes 49160 | tf_op jit(solution)/shard_map/ppermute | solution.py:20
  182.6 5.1 %collective-permute-start.13 = (f32[1,16,256]{2,1,0:T(8,128)S(1)}, f32[1,16,256]{2,1,0:T(8,128)S(1)}, u32[]{:S(2)}, u32[]{:S(2)}) collective-permute-start(f32[1,16,256]{2,1,0:T(8,128)S(1)} %get-tuple-element.106), channel_id=1, source_target_pairs={{16,0},{32,16},{48,32},{64,48},{80,64},{96,80},{112,96},{17,1},{33... | collective-permute-start | bytes 49160 | tf_op jit(solution)/shard_map/ppermute | solution.py:21
  187.7 6.0 %collective-permute-start.14 = (f32[18,1,256]{2,1,0:T(1,128)S(1)}, f32[18,1,256]{2,1,0:T(1,128)S(1)}, u32[]{:S(2)}, u32[]{:S(2)}) collective-permute-start(f32[18,1,256]{2,1,0:T(1,128)S(1)} %get-tuple-element.99), channel_id=1, source_target_pairs={{0,4},{4,8},{8,12},{1,5},{5,9},{9,13},{2,6},{6,10},{10,14},{3,7},{... | collective-permute-start | bytes 55304 | tf_op jit(solution)/shard_map/ppermute | solution.py:20
  191.9 4.9 %collective-permute-start.15 = (f32[18,1,256]{2,1,0:T(1,128)S(1)}, f32[18,1,256]{2,1,0:T(1,128)S(1)}, u32[]{:S(2)}, u32[]{:S(2)}) collective-permute-start(f32[18,1,256]{2,1,0:T(1,128)S(1)} %get-tuple-element.100), channel_id=1, source_target_pairs={{4,0},{8,4},{12,8},{5,1},{9,5},{13,9},{6,2},{10,6},{14,10},{7,3},{... | collective-permute-start | bytes 55304 | tf_op jit(solution)/shard_map/ppermute | solution.py:21
  197.7 9.0 %collective-permute-start.16 = (f32[18,18,1]{2,1,0:T(8,128)}, f32[18,18,1]{2,1,0:T(8,128)}, u32[]{:S(2)}, u32[]{:S(2)}) collective-permute-start(f32[18,18,1]{2,1,0:T(8,128)} %get-tuple-element.91), channel_id=1, source_target_pairs={{0,1},{1,2},{2,3},{4,5},{5,6},{6,7},{8,9},{9,10},{10,11},{12,13},{... | collective-permute-start | bytes 3896 | tf_op jit(solution)/shard_map/ppermute | solution.py:20
  202.7 8.6 %collective-permute-start.17 = (f32[18,18,1]{2,1,0:T(8,128)}, f32[18,18,1]{2,1,0:T(8,128)}, u32[]{:S(2)}, u32[]{:S(2)}) collective-permute-start(f32[18,18,1]{2,1,0:T(8,128)} %get-tuple-element.92), channel_id=1, source_target_pairs={{1,0},{2,1},{3,2},{5,4},{6,5},{7,6},{9,8},{10,9},{11,10},{13,12},{... | collective-permute-start | bytes 3896 | tf_op jit(solution)/shard_map/ppermute | solution.py:21
  274.2 4.5 %collective-permute-start.18 = (f32[2,16,256]{2,1,0:T(8,128)}, f32[2,16,256]{2,1,0:T(8,128)S(1)}, u32[]{:S(2)}, u32[]{:S(2)}) collective-permute-start(f32[2,16,256]{2,1,0:T(8,128)} %get-tuple-element.103), channel_id=1, source_target_pairs={{0,16},{16,32},{32,48},{48,64},{64,80},{80,96},{96,112},{1,17},{17... | collective-permute-start | bytes 98312 | tf_op jit(solution)/shard_map/ppermute | solution.py:20
  276.2 5.4 %collective-permute-start.19 = (f32[2,16,256]{2,1,0:T(8,128)}, f32[2,16,256]{2,1,0:T(8,128)S(1)}, u32[]{:S(2)}, u32[]{:S(2)}) collective-permute-start(f32[2,16,256]{2,1,0:T(8,128)} %get-tuple-element.104), channel_id=1, source_target_pairs={{16,0},{32,16},{48,32},{64,48},{80,64},{96,80},{112,96},{17,1},{33... | collective-permute-start | bytes 98312 | tf_op jit(solution)/shard_map/ppermute | solution.py:21
  282.6 3.9 collective-permute-start.20
  285.0 4.7 %collective-permute-start.21 = (f32[20,2,256]{2,1,0:T(2,128)S(1)}, f32[20,2,256]{2,1,0:T(2,128)S(1)}, u32[]{:S(2)}, u32[]{:S(2)}) collective-permute-start(f32[20,2,256]{2,1,0:T(2,128)S(1)} %get-tuple-element.94), channel_id=1, source_target_pairs={{4,0},{8,4},{12,8},{5,1},{9,5},{13,9},{6,2},{10,6},{14,10},{7,3},{... | collective-permute-start | bytes 122888 | tf_op jit(solution)/shard_map/ppermute | solution.py:21
  290.9 10.9 %collective-permute-start.22 = (f32[20,20,2]{2,1,0:T(8,128)S(1)}, f32[20,20,2]{2,1,0:T(8,128)S(1)}, u32[]{:S(2)}, u32[]{:S(2)}) collective-permute-start(f32[20,20,2]{2,1,0:T(8,128)S(1)} %get-tuple-element.85), channel_id=1, source_target_pairs={{0,1},{1,2},{2,3},{4,5},{5,6},{6,7},{8,9},{9,10},{10,11},{12,13},{... | collective-permute-start | bytes 9608 | tf_op jit(solution)/shard_map/ppermute | solution.py:20
  293.9 9.4 %collective-permute-start.23 = (f32[20,20,2]{2,1,0:T(8,128)S(1)}, f32[20,20,2]{2,1,0:T(8,128)S(1)}, u32[]{:S(2)}, u32[]{:S(2)}) collective-permute-start(f32[20,20,2]{2,1,0:T(8,128)S(1)} %get-tuple-element.86), channel_id=1, source_target_pairs={{1,0},{2,1},{3,2},{5,4},{6,5},{7,6},{9,8},{10,9},{11,10},{13,12},{... | collective-permute-start | bytes 9608 | tf_op jit(solution)/shard_map/ppermute | solution.py:21
  311.6 4.4 %collective-permute-start.24 = (f32[1,16,256]{2,1,0:T(8,128)S(1)}, f32[1,16,256]{2,1,0:T(8,128)S(1)}, u32[]{:S(2)}, u32[]{:S(2)}) collective-permute-start(f32[1,16,256]{2,1,0:T(8,128)S(1)} %get-tuple-element.101), channel_id=1, source_target_pairs={{0,16},{16,32},{32,48},{48,64},{64,80},{80,96},{96,112},{1,17},{17... | collective-permute-start | bytes 49160 | tf_op jit(solution)/shard_map/ppermute | solution.py:20
  314.0 5.1 %collective-permute-start.25 = (f32[1,16,256]{2,1,0:T(8,128)S(1)}, f32[1,16,256]{2,1,0:T(8,128)S(1)}, u32[]{:S(2)}, u32[]{:S(2)}) collective-permute-start(f32[1,16,256]{2,1,0:T(8,128)S(1)} %get-tuple-element.102), channel_id=1, source_target_pairs={{16,0},{32,16},{48,32},{64,48},{80,64},{96,80},{112,96},{17,1},{33... | collective-permute-start | bytes 49160 | tf_op jit(solution)/shard_map/ppermute | solution.py:21
  319.1 4.1 %collective-permute-start.26 = (f32[18,1,256]{2,1,0:T(1,128)S(1)}, f32[18,1,256]{2,1,0:T(1,128)S(1)}, u32[]{:S(2)}, u32[]{:S(2)}) collective-permute-start(f32[18,1,256]{2,1,0:T(1,128)S(1)} %get-tuple-element.97), channel_id=1, source_target_pairs={{0,4},{4,8},{8,12},{1,5},{5,9},{9,13},{2,6},{6,10},{10,14},{3,7},{... | collective-permute-start | bytes 55304 | tf_op jit(solution)/shard_map/ppermute | solution.py:20
  321.9 4.5 %collective-permute-start.27 = (f32[18,1,256]{2,1,0:T(1,128)S(1)}, f32[18,1,256]{2,1,0:T(1,128)S(1)}, u32[]{:S(2)}, u32[]{:S(2)}) collective-permute-start(f32[18,1,256]{2,1,0:T(1,128)S(1)} %get-tuple-element.98), channel_id=1, source_target_pairs={{4,0},{8,4},{12,8},{5,1},{9,5},{13,9},{6,2},{10,6},{14,10},{7,3},{... | collective-permute-start | bytes 55304 | tf_op jit(solution)/shard_map/ppermute | solution.py:21
  326.6 9.4 %collective-permute-start.28 = (f32[18,18,1]{2,1,0:T(8,128)S(1)}, f32[18,18,1]{2,1,0:T(8,128)S(1)}, u32[]{:S(2)}, u32[]{:S(2)}) collective-permute-start(f32[18,18,1]{2,1,0:T(8,128)S(1)} %get-tuple-element.89), channel_id=1, source_target_pairs={{0,1},{1,2},{2,3},{4,5},{5,6},{6,7},{8,9},{9,10},{10,11},{12,13},{... | collective-permute-start | bytes 3896 | tf_op jit(solution)/shard_map/ppermute | solution.py:20
  330.8 9.1 %collective-permute-start.29 = (f32[18,18,1]{2,1,0:T(8,128)S(1)}, f32[18,18,1]{2,1,0:T(8,128)S(1)}, u32[]{:S(2)}, u32[]{:S(2)}) collective-permute-start(f32[18,18,1]{2,1,0:T(8,128)S(1)} %get-tuple-element.90), channel_id=1, source_target_pairs={{1,0},{2,1},{3,2},{5,4},{6,5},{7,6},{9,8},{10,9},{11,10},{13,12},{... | collective-permute-start | bytes 3896 | tf_op jit(solution)/shard_map/ppermute | solution.py:21
  (35 other events, 752.6 us)
